TPU v7x, 32 devices: a whole 2x2x4 slice. The times are simulated.
32 devices in a mesh: row: 2 (over x), col: 4 (over z), depth: 4 (over y, core).
Axes of the slice: x: 2, y: 2, z: 4, core: 2. Of those that a mesh axis runs over, the one named last changes fastest.
Arguments:
- trailing: float32 [8192, 8192], P('row', 'col'), may hold values from -6 to 6
- panel: bfloat16 [8192, 4096], P('row', 'col'), may hold values from -0.75 to 0.75
- inverse_factor: bfloat16 [4096, 4096], P('depth', 'col'), may hold values from -0.09375 to 0.09375
- block_inverse: float32 [8192, 512], P('row'), may hold values from -0.25 to 0.25
- guess: float32 [8192, 128], P(('col', 'depth')), may hold values from -0.0625 to 0.0625
- target: float32 [8192, 128], P('row'), may hold values from -6 to 6
Outputs:
- updated: float32 [8192, 8192], P('row', ('col', 'depth'))
- correction: float32 [8192, 128], P('row')
- residual_rms: float32 [1], replicated
All inputs are finite; a program needn't handle non-finite values.
Results may differ from a plain program's by a relative error of at most 0.00036.
Values may be sent and summed in bfloat16 or wider, within the bound.
A program may use at most 192 MiB of HBM per device.

v0:
```python
import jax
import jax.numpy as jnp
from jax import lax
from jax.sharding import PartitionSpec as P

N = 8192
BS = 512
R = 128


def body(trailing, panel, inverse_factor, block_inverse, guess, target):
    rows_here = panel.shape[0]
    cols_here = trailing.shape[1]
    width_k = inverse_factor.shape[0]
    width_j = inverse_factor.shape[1]
    row_id = lax.axis_index("row")
    col_id = lax.axis_index("col")
    depth_id = lax.axis_index("depth")
    k_index = depth_id * width_k + lax.broadcasted_iota(jnp.int32, (width_k, width_j), 0)
    j_index = col_id * width_j + lax.broadcasted_iota(jnp.int32, (width_k, width_j), 1)
    lower = jnp.where(k_index >= j_index, inverse_factor, jnp.zeros_like(inverse_factor))
    partial_value = lax.dot_general(
        panel, lower, (((1,), (1,)), ((), ())), preferred_element_type=jnp.float32
    )
    share = lax.psum_scatter(partial_value, "col", scatter_dimension=0, tiled=True)
    everything = lax.all_gather(share.astype(jnp.bfloat16), ("row", "col"), axis=0, tiled=True)
    factor_rows = lax.dynamic_slice_in_dim(everything, row_id * rows_here, rows_here, 0)
    factor_cols = lax.dynamic_slice_in_dim(everything, col_id * cols_here, cols_here, 0)
    share_cols = cols_here // lax.axis_size("depth")
    product = lax.dot_general(
        factor_rows, factor_cols, (((1,), (1,)), ((), ())), preferred_element_type=jnp.float32
    )
    total = lax.psum_scatter(product, "depth", scatter_dimension=1, tiled=True)
    mine = lax.dynamic_slice_in_dim(trailing, depth_id * share_cols, share_cols, 1)
    updated = mine - total
    applied = jnp.dot(
        updated, guess, precision=lax.Precision.HIGHEST, preferred_element_type=jnp.float32
    )
    applied = lax.psum(applied, ("col", "depth"))
    residual = target - applied
    squares = lax.psum(jnp.sum(residual * residual), "row")
    residual_rms = jnp.sqrt(squares / (N * R))
    count = rows_here // BS
    blocks = jnp.tril(block_inverse.reshape(count, BS, BS))
    pieces = residual.reshape(count, BS, residual.shape[1])
    first = jnp.einsum("bij,bjr->bir", blocks, pieces, precision=lax.Precision.HIGHEST)
    second = jnp.einsum("bji,bjr->bir", blocks, first, precision=lax.Precision.HIGHEST)
    correction = second.reshape(rows_here, residual.shape[1])
    return (updated, correction, residual_rms.reshape(1))


def solution(mesh):
    placed = (
        P("row", "col"),
        P("row", "col"),
        P("depth", "col"),
        P("row", None),
        P(("col", "depth"), None),
        P("row", None),
    )
    return jax.shard_map(
        body,
        mesh=mesh,
        in_specs=placed,
        out_specs=(P("row", ("col", "depth")), P("row", None), P()),
        check_vma=False,
    )
```

profile of v0, /device:TPU:0, one launch (start us, length us, event | category | flops | bytes accessed | tf_op | source)
XLA Modules:
  0.0 956.3 jit_solution(15078148875091785911)
XLA Ops:
  7.2 0.0 copy-start
  7.2 0.0 reduce-scatter.3.cloned.1.call-start
  7.2 16.3 %convolution_bitcast_fusion = f32[4096,1024]{0,1:T(8,128)} fusion(bf16[4096,1024]{1,0:T(8,128)(2,1)} %param.7, bf16[1024,1024]{1,0:T(8,128)(2,1)} %param.8, s32[1024]{0:T(1024)S(1)} %get-tuple-element.5, s32[1024]{0:T(1024)S(1)} %get-tuple-element.6), kind=kOutput, calls=%fused_computation | convolution fusion | flops 8592031744 | bytes 27271168 | tf_op jit(solution)/shard_map/dot_general | solution.py:22
  23.5 0.0 reduce-scatter.3.cloned.1.call-update
  23.5 0.0 all-gather.2.cloned.1.call-start
  23.6 283.3 %reduce-scatter.3.cloned.1.call-done = f32[1024,1024]{0,1:T(8,128)} async-done(((f32[4096,1024]{0,1:T(8,128)}), f32[1024,1024]{0,1:T(8,128)}) %reduce-scatter.3.cloned.1.call-update) | async-done | bytes 4194320 | tf_op jit(solution)/shard_map/reduce_scatter | solution.py:25
  306.9 3.8 convert_element_type.3
  310.7 0.0 all-gather.2.cloned.1.call-update
  310.7 0.0 reduce-scatter.5.cloned.1.call-start
  310.8 228.0 %all-gather.2.cloned.1.call-done = bf16[8192,1024]{0,1:T(8,128)(2,1)} async-done(((bf16[1024,1024]{0,1:T(8,128)(2,1)}), bf16[8192,1024]{0,1:T(8,128)(2,1)}) %all-gather.2.cloned.1.call-update) | async-done | bytes 16777232 | tf_op jit(solution)/shard_map/all_gather | solution.py:26
  538.8 25.5 %fusion = f32[4096,2048]{1,0:T(8,128)} fusion(bf16[8192,1024]{0,1:T(8,128)(2,1)} %all-gather.2.cloned.1.call-done, s32[]{:T(128)S(6)} %select_n.19, s32[]{:T(128)S(6)} %select_n.20), kind=kOutput, calls=%fused_computation.1 | convolution fusion | flops 17179869184 | bytes 46137352 | tf_op jit(solution)/shard_map/dot_general | solution.py:30
  564.3 0.0 reduce-scatter.5.cloned.1.call-update
  564.3 0.0 all-reduce.2.cloned.1.call-start
  564.4 230.4 %reduce-scatter.5.cloned.1.call-done = f32[4096,512]{1,0:T(8,128)} async-done(((f32[4096,2048]{1,0:T(8,128)}), f32[4096,512]{1,0:T(8,128)}) %reduce-scatter.5.cloned.1.call-update) | async-done | bytes 8388624 | tf_op jit(solution)/shard_map/reduce_scatter | solution.py:33
  794.8 11.3 %dynamic-slice_subtract_fusion = f32[4096,512]{1,0:T(8,128)} fusion(f32[4096,512]{1,0:T(8,128)} %reduce-scatter.5.cloned.1.call-done, f32[4096,2048]{1,0:T(8,128)} %param.6, s32[]{:T(128)S(6)} %select_n.17), kind=kLoop, calls=%fused_computation.3 | loop fusion | flops 2097152 | bytes 25165828 | tf_op jit(solution)/shard_map/sub | solution.py:35
  806.1 10.1 %fusion.18 = f32[4096,128]{1,0:T(8,128)} fusion(f32[4096,512]{1,0:T(8,128)} %dynamic-slice_subtract_fusion, f32[512,128]{1,0:T(8,128)S(1)} %copy-done), kind=kOutput, calls=%fused_computation.25 | convolution fusion | flops 3221225472 | bytes 10747904 | tf_op jit(solution)/shard_map/dot_general | solution.py:36
  816.2 0.0 all-reduce.2.cloned.1.call-update
  816.2 9.3 copy.9
  825.5 0.1 iota_compare_fusion
  825.6 88.8 %all-reduce.2.cloned.1.call-done = f32[4096,128]{1,0:T(8,128)} async-done(((f32[4096,128]{1,0:T(8,128)}), f32[4096,128]{1,0:T(8,128)}) %all-reduce.2.cloned.1.call-update) | async-done | bytes 2097168 | tf_op jit(solution)/shard_map/psum | solution.py:39
  914.4 2.9 multiply_reduce_fusion
  917.3 16.1 %fusion.4 = f32[8,512,128]{2,1,0:T(8,128)S(1)} fusion(f32[8,512,128]{2,1,0:T(8,128)S(1)} %bitcast.13, f32[8,512,512]{1,2,0:T(8,128)} %copy.9, pred[512,512]{0,1:T(8,128)(4,1)S(1)} %iota_compare_fusion), kind=kOutput, calls=%fused_computation.6 | convolution fusion | flops 3223322624 | bytes 12845056 | tf_op jit(solution)/shard_map/bij,bjr->bir/dot_general | solution.py:46
  933.4 9.0 fusion.2
  942.4 5.5 psum.15
  (9 shorter events, 0.0 us)
Async XLA Ops:
  7.2 798.9 %copy-start = (f32[512,128]{1,0:T(8,128)S(1)}, f32[512,128]{1,0:T(8,128)}, u32[]{:S(2)}) copy-start(f32[512,128]{1,0:T(8,128)} %param.10) | copy-start | bytes 786436
  7.2 299.7 %reduce-scatter.3.cloned.1.call-start = ((), (), s32[]{:S(2)}) async-start(), calls=%async_computation.2 | async-start | bytes 20971520 | tf_op jit(solution)/shard_map/reduce_scatter | solution.py:25
  23.5 515.2 %all-gather.2.cloned.1.call-start = ((), (), s32[]{:S(2)}) async-start(), calls=%async_computation.3 | async-start | bytes 18874368 | tf_op jit(solution)/shard_map/all_gather | solution.py:26
  310.7 484.1 %reduce-scatter.5.cloned.1.call-start = ((), (), s32[]{:S(2)}) async-start(), calls=%async_computation.4 | async-start | bytes 41943040 | tf_op jit(solution)/shard_map/reduce_scatter | solution.py:33
  564.3 350.1 %all-reduce.2.cloned.1.call-start = ((), (), s32[]{:S(2)}) async-start(), calls=%async_computation.5 | async-start | bytes 4194304 | tf_op jit(solution)/shard_map/psum | solution.py:39
  816.2 98.2 %copy-start.1 = (f32[4096,128]{1,0:T(8,128)S(1)}, f32[4096,128]{1,0:T(8,128)}, u32[]{:S(2)}) copy-start(f32[4096,128]{1,0:T(8,128)} %param.11) | copy-start | bytes 6291460
  914.4 19.0 %slice-start = ((s8[8388608]{0:T(1024)(128)(4,1)}), s8[4194304]{0:T(1024)(128)(4,1)S(1)}, s32[]{:S(2)}) async-start(s8[8388608]{0:T(1024)(128)(4,1)} %bitcast.11), calls=%async_computation.6 | async-start | bytes 8388608
  917.3 16.1 %slice-start.1 = ((s8[8388608]{0:T(1024)(128)(4,1)}), s8[4194304]{0:T(1024)(128)(4,1)S(1)}, s32[]{:S(2)}) async-start(s8[8388608]{0:T(1024)(128)(4,1)} %bitcast.11), calls=%async_computation.7 | async-start | bytes 8388608
Sparse Core Ops, SparseCore 0:
  23.7 283.1 reduce-scatter.2
  310.8 227.8 all-gather.1
  564.5 230.3 reduce-scatter.4
  816.3 98.0 all-reduce.1
where the time goes:
time: 957 us; the launch traced here: 956 us
  waiting for transfers between devices  831 us (87%)
  matrix products  77 us (8%)
  other arithmetic  18.1 us (2%)
  between operations  15.7 us (2%)
    reduce_scatter x1, waiting for transfers between devices, body(): lax.psum_scatter(partial_value, 'col', scatter_dimension=0, tiled=True)  283 us
    reduce_scatter x1, waiting for transfers between devices, body(): total = lax.psum_scatter(product, 'depth', scatter_dimension=1, tiled=True)  230 us
    all_gather x1, waiting for transfers between devices, body(): lax.all_gather(share.astype(jnp.bfloat16), ('row', 'col'), axis=0, tiled=...  228 us
    psum x1, waiting for transfers between devices, body(): applied = lax.psum(applied, ('col', 'depth'))  88.8 us
    dot_general x1, matrix products, body(): lax.dot_general(factor_rows, factor_cols, (((1,), (1,)), ((), ())), prefe...  25.5 us
  transfers between devices with their start and end apart: 4, of which 4 were waited for; matrix products, arithmetic and copies ran while one was open for 1% of the time, Pallas kernels for 0%

commit v1 on v0

--- a/solution.py
+++ b/solution.py
@@ -36,7 +36,7 @@
     applied = jnp.dot(
         updated, guess, precision=lax.Precision.HIGHEST, preferred_element_type=jnp.float32
     )
-    applied = lax.psum(applied, ("col", "depth"))
+    applied = lax.psum(lax.psum(applied, "depth"), "col")
     residual = target - applied
     squares = lax.psum(jnp.sum(residual * residual), "row")
     residual_rms = jnp.sqrt(squares / (N * R))

time: 957 us -> 998 us (1.043)
  waiting for transfers between devices: 831 us -> 872 us
    psum x1 -> x2, waiting for transfers between devices: 88.8 us -> 130 us  [body(): applied = lax.psum(lax.psum(applied, 'depth'), 'col')]
  transfers between devices with their start and end apart: 4 -> 5, of which waited for: 4 -> 5; matrix products, arithmetic and copies ran while one was open for 1% -> 1% of each run, Pallas kernels for 0% -> 0%
where the time goes in v1:
time: 998 us
  waiting for transfers between devices  872 us (87%)
  matrix products  77 us (8%)
  other arithmetic  18.1 us (2%)
  between operations  15.7 us (2%)
    reduce_scatter x1, waiting for transfers between devices, body(): lax.psum_scatter(partial_value, 'col', scatter_dimension=0, tiled=True)  283 us
    reduce_scatter x1, waiting for transfers between devices, body(): total = lax.psum_scatter(product, 'depth', scatter_dimension=1, tiled=True)  230 us
    all_gather x1, waiting for transfers between devices, body(): lax.all_gather(share.astype(jnp.bfloat16), ('row', 'col'), axis=0, tiled=...  228 us
    psum x2, waiting for transfers between devices, body(): applied = lax.psum(lax.psum(applied, 'depth'), 'col')  130 us
    dot_general x1, matrix products, body(): lax.dot_general(factor_rows, factor_cols, (((1,), (1,)), ((), ())), prefe...  25.5 us
  transfers between devices with their start and end apart: 5, of which 5 were waited for; matrix products, arithmetic and copies ran while one was open for 1% of the time, Pallas kernels for 0%

profile of v1, /device:TPU:0, one launch (start us, length us, event | category | flops | bytes accessed | tf_op | source)
XLA Modules:
  0.0 998.1 jit_solution(12481906959672289504)
XLA Ops:
  7.2 0.0 reduce-scatter.3.cloned.1.call-start
  7.2 16.3 %convolution_bitcast_fusion = f32[4096,1024]{0,1:T(8,128)} fusion(bf16[4096,1024]{1,0:T(8,128)(2,1)} %param.7, bf16[1024,1024]{1,0:T(8,128)(2,1)} %param.8, s32[1024]{0:T(1024)S(1)} %get-tuple-element.5, s32[1024]{0:T(1024)S(1)} %get-tuple-element.6), kind=kOutput, calls=%fused_computation | convolution fusion | flops 8592031744 | bytes 27271168 | tf_op jit(solution)/shard_map/dot_general | solution.py:22
  23.5 0.0 reduce-scatter.3.cloned.1.call-update
  23.5 0.0 all-gather.2.cloned.1.call-start
  23.6 283.3 %reduce-scatter.3.cloned.1.call-done = f32[1024,1024]{0,1:T(8,128)} async-done(((f32[4096,1024]{0,1:T(8,128)}), f32[1024,1024]{0,1:T(8,128)}) %reduce-scatter.3.cloned.1.call-update) | async-done | bytes 4194320 | tf_op jit(solution)/shard_map/reduce_scatter | solution.py:25
  306.9 3.8 convert_element_type.3
  310.7 0.0 reduce-scatter.5.cloned.1.call-start
  310.8 228.0 %all-gather.2.cloned.1.call-done = bf16[8192,1024]{0,1:T(8,128)(2,1)} async-done(((bf16[1024,1024]{0,1:T(8,128)(2,1)}), bf16[8192,1024]{0,1:T(8,128)(2,1)}) %all-gather.2.cloned.1.call-update) | async-done | bytes 16777232 | tf_op jit(solution)/shard_map/all_gather | solution.py:26
  538.8 25.5 %fusion = f32[4096,2048]{1,0:T(8,128)} fusion(bf16[8192,1024]{0,1:T(8,128)(2,1)} %all-gather.2.cloned.1.call-done, s32[]{:T(128)S(6)} %select_n.19, s32[]{:T(128)S(6)} %select_n.20), kind=kOutput, calls=%fused_computation.1 | convolution fusion | flops 17179869184 | bytes 46137352 | tf_op jit(solution)/shard_map/dot_general | solution.py:30
  564.3 0.0 reduce-scatter.5.cloned.1.call-update
  564.3 0.2 all-reduce.3.cloned.1.call-start
  564.6 230.3 %reduce-scatter.5.cloned.1.call-done = f32[4096,512]{1,0:T(8,128)} async-done(((f32[4096,2048]{1,0:T(8,128)}), f32[4096,512]{1,0:T(8,128)}) %reduce-scatter.5.cloned.1.call-update) | async-done | bytes 8388624 | tf_op jit(solution)/shard_map/reduce_scatter | solution.py:33
  794.8 11.3 %dynamic-slice_subtract_fusion = f32[4096,512]{1,0:T(8,128)} fusion(f32[4096,512]{1,0:T(8,128)} %reduce-scatter.5.cloned.1.call-done, f32[4096,2048]{1,0:T(8,128)} %param.6, s32[]{:T(128)S(6)} %select_n.17), kind=kLoop, calls=%fused_computation.3 | loop fusion | flops 2097152 | bytes 25165828 | tf_op jit(solution)/shard_map/sub | solution.py:35
  806.1 10.1 %fusion.18 = f32[4096,128]{1,0:T(8,128)} fusion(f32[4096,512]{1,0:T(8,128)} %dynamic-slice_subtract_fusion, f32[512,128]{1,0:T(8,128)S(1)} %copy-done), kind=kOutput, calls=%fused_computation.25 | convolution fusion | flops 3221225472 | bytes 10747904 | tf_op jit(solution)/shard_map/dot_general | solution.py:36
  816.1 0.0 all-reduce.3.cloned.1.call-update
  816.2 0.3 all-reduce.5.cloned.1.call-start
  816.4 51.3 %all-reduce.3.cloned.1.call-done = f32[4096,128]{1,0:T(8,128)} async-done(((f32[4096,128]{1,0:T(8,128)}), f32[4096,128]{1,0:T(8,128)}) %all-reduce.3.cloned.1.call-update) | async-done | bytes 2097168 | tf_op jit(solution)/shard_map/psum | solution.py:39
  867.8 9.4 copy.9
  877.1 0.1 iota_compare_fusion
  877.2 78.9 %all-reduce.5.cloned.1.call-done = f32[4096,128]{1,0:T(8,128)} async-done(((f32[4096,128]{1,0:T(8,128)}), f32[4096,128]{1,0:T(8,128)}) %all-reduce.5.cloned.1.call-update) | async-done | bytes 2097168 | tf_op jit(solution)/shard_map/psum | solution.py:39
  956.2 2.9 multiply_reduce_fusion
  959.1 16.1 %fusion.4 = f32[8,512,128]{2,1,0:T(8,128)S(1)} fusion(f32[8,512,128]{2,1,0:T(8,128)S(1)} %bitcast.13, f32[8,512,512]{1,2,0:T(8,128)} %copy.9, pred[512,512]{0,1:T(8,128)(4,1)S(1)} %iota_compare_fusion), kind=kOutput, calls=%fused_computation.6 | convolution fusion | flops 3223322624 | bytes 12845056 | tf_op jit(solution)/shard_map/bij,bjr->bir/dot_general | solution.py:46
  975.2 9.0 fusion.2
  984.3 5.5 psum.23
  (12 shorter events, 0.1 us)
Async XLA Ops:
  7.2 798.9 %copy-start = (f32[512,128]{1,0:T(8,128)S(1)}, f32[512,128]{1,0:T(8,128)}, u32[]{:S(2)}) copy-start(f32[512,128]{1,0:T(8,128)} %param.10) | copy-start | bytes 786436
  7.2 299.7 %reduce-scatter.3.cloned.1.call-start = ((), (), s32[]{:S(2)}) async-start(), calls=%async_computation.2 | async-start | bytes 20971520 | tf_op jit(solution)/shard_map/reduce_scatter | solution.py:25
  23.5 515.2 %all-gather.2.cloned.1.call-start = ((), (), s32[]{:S(2)}) async-start(), calls=%async_computation.3 | async-start | bytes 18874368 | tf_op jit(solution)/shard_map/all_gather | solution.py:26
  310.7 484.1 %reduce-scatter.5.cloned.1.call-start = ((), (), s32[]{:S(2)}) async-start(), calls=%async_computation.4 | async-start | bytes 41943040 | tf_op jit(solution)/shard_map/reduce_scatter | solution.py:33
  564.3 303.4 %all-reduce.3.cloned.1.call-start = ((), (), s32[]{:S(2)}) async-start(), calls=%async_computation.5 | async-start | bytes 4194304 | tf_op jit(solution)/shard_map/psum | solution.py:39
  816.2 140.0 %all-reduce.5.cloned.1.call-start = ((), (), s32[]{:S(2)}) async-start(), calls=%async_computation.6 | async-start | bytes 4194304 | tf_op jit(solution)/shard_map/psum | solution.py:39
  867.7 88.4 %copy-start.1 = (f32[4096,128]{1,0:T(8,128)S(1)}, f32[4096,128]{1,0:T(8,128)}, u32[]{:S(2)}) copy-start(f32[4096,128]{1,0:T(8,128)} %param.11) | copy-start | bytes 6291460
  956.2 19.0 %slice-start = ((s8[8388608]{0:T(1024)(128)(4,1)}), s8[4194304]{0:T(1024)(128)(4,1)S(1)}, s32[]{:S(2)}) async-start(s8[8388608]{0:T(1024)(128)(4,1)} %bitcast.11), calls=%async_computation.7 | async-start | bytes 8388608
  959.1 16.1 %slice-start.1 = ((s8[8388608]{0:T(1024)(128)(4,1)}), s8[4194304]{0:T(1024)(128)(4,1)S(1)}, s32[]{:S(2)}) async-start(s8[8388608]{0:T(1024)(128)(4,1)} %bitcast.11), calls=%async_computation.8 | async-start | bytes 8388608
Sparse Core Ops, SparseCore 0:
  23.7 283.1 reduce-scatter.2
  310.8 227.8 all-gather.1
  564.5 230.3 reduce-scatter.4
  816.3 51.3 all-reduce.2
  869.9 86.1 all-reduce.4
